TPU v7x, 512 devices: a whole 4x4x16 slice. The times are simulated.
512 devices in a mesh: cell: 32 (over x, y, core), blk: 16 (over z).
Axes of the slice: x: 4, y: 4, z: 16, core: 2. Of those that a mesh axis runs over, the one named last changes fastest.
Arguments:
- snapshots: float32 [512, 65536], P('blk', 'cell'), may hold values from -100 to 100
- plan: int32 [31, 32], replicated, may hold values from 0 to 31, as said below
Outputs:
- energy_field: float32 [512, 65536], P('blk', 'cell')
- mode_energy: float32 [512], P('blk')
Inputs may be any that keep to these rules, and one draw needn't show every extreme that they name: `plan`: each row pairs every index 0 .. 31 with exactly one other index (the partner's partner is the index itself, never the index), and over all rows every two indices are paired exactly once.
All inputs are finite; a program needn't handle non-finite values.
Results may differ from a plain program's by a relative error of at most 0.0055.
Values sent between devices are 32-bit elements; how exact they have to be, the bound alone decides.
A program may use at most 64 MiB of HBM per device.

v0:
```python
import jax
import jax.numpy as jnp
from jax import lax
from jax.sharding import PartitionSpec as P

ROUNDS = 7


def passed_along(value, axis, steps):
    count = lax.axis_size(axis)
    first, last = (max(0, -steps), min(count, count - steps))
    return lax.ppermute(value, axis, [(source, source + steps) for source in range(first, last)])


def inner_sweep(gram_whole, plan):
    pair_width = gram_whole.shape[0]
    positions = jnp.arange(pair_width, dtype=jnp.int32)

    def one_step(step_index, loop_state):
        gram_now, accumulated = loop_state
        partner = lax.dynamic_index_in_dim(plan, step_index, 0, keepdims=False)
        onehot = (partner[:, None] == positions[None, :]).astype(jnp.float32)
        symmetric = 0.5 * (gram_now + gram_now.T)
        own_diag = jnp.diagonal(symmetric)
        cross_term = jnp.sum(onehot * symmetric, axis=1)
        other_diag = jnp.sum(onehot * own_diag[None, :], axis=1)
        is_lower = positions < partner
        spread = jnp.where(is_lower, own_diag - other_diag, other_diag - own_diag)
        angles = 0.5 * jnp.arctan2(2.0 * cross_term, spread)
        cosine = jnp.cos(angles)
        sine_part = jnp.where(is_lower, jnp.sin(angles), -jnp.sin(angles))
        rotation_step = jnp.diag(cosine) + (onehot * sine_part[:, None]).T
        gram_now = jnp.dot(
            jnp.dot(rotation_step.T, gram_now, precision=lax.Precision.HIGHEST),
            rotation_step,
            precision=lax.Precision.HIGHEST,
        )
        accumulated = jnp.dot(accumulated, rotation_step, precision=lax.Precision.HIGHEST)
        return (gram_now, accumulated)

    initial = (gram_whole, jnp.eye(pair_width, dtype=jnp.float32))
    return lax.fori_loop(0, pair_width - 1, one_step, initial)[1]


def self_gram(block):
    return jnp.dot(block, block.T, precision=lax.Precision.HIGHEST)


def on_device(snapshots, plan):
    pair_width = snapshots.shape[0]
    half_width = pair_width // 2
    local_rows = snapshots.shape[1]
    block_devices = lax.axis_size("blk")
    position = lax.axis_index("blk")

    def round_step(round_index, loop_state):
        current, gram_local = loop_state
        gram_whole = lax.psum(gram_local, "cell")
        turning = inner_sweep(gram_whole, plan)
        rotated = jnp.dot(turning.T, current, precision=lax.Precision.HIGHEST)
        upper_part = rotated[:half_width]
        lower_part = rotated[half_width:]
        rightward = jnp.where(position == 0, lower_part, upper_part)
        from_left = passed_along(rightward, "blk", 1)
        from_right = passed_along(lower_part, "blk", -1)
        new_upper = jnp.where(position == 0, upper_part, from_left)
        new_lower = jnp.where(position == block_devices - 1, upper_part, from_right)
        current = jnp.concatenate([new_upper, new_lower], axis=0)
        gram_local = self_gram(current)
        return (current, gram_local)

    gram_first = self_gram(snapshots)
    current, gram_local = lax.fori_loop(0, ROUNDS, round_step, (snapshots, gram_first))
    squared = current * current
    energy_local = jnp.sum(squared, axis=1)
    total_rows = local_rows * lax.axis_size("cell")
    mode_energy = lax.psum(energy_local, "cell") / total_rows
    return (squared, mode_energy)


def solution(mesh):
    return jax.shard_map(
        on_device,
        mesh=mesh,
        in_specs=(P("blk", "cell"), P()),
        out_specs=(P("blk", "cell"), P("blk")),
        check_vma=False,
    )
```

profile of v0, /device:TPU:1, one launch (start us, length us, event | category | flops | bytes accessed | tf_op | source)
XLA Modules:
  0.0 1892.4 jit_solution(1336124570133756698)
XLA Ops:
  1.9 1820.3 %while.37 = (s32[]{:T(128)}, f32[32,2048]{1,0:T(8,128)S(1)}, f32[32,32]{1,0:T(8,128)S(1)}, pred[]{:T(512)}, s32[31,32]{1,0:T(8,128)}, /*index=5*/pred[]{:T(512)}, s32[]{:T(128)}, s32[]{:T(128)}, s32[]{:T(128)}) while((s32[]{:T(128)}, f32[32,2048]{1,0:T(8,128)S(1)}, f32[32,32]{1,0:T(8,128)S(1)}, pred[]{:T(512)}, s32[31,32]{1,0:T(8,128)}, ...), condition=%wide.region_6.7_spmd, body=%wide.region_0.6_spmd.sunk | while | flops 51701092 | bytes 3620785 | solution.py:73
  2.0 125.0 %psum.18 = f32[32,32]{1,0:T(8,128)S(1)} all-reduce(f32[32,32]{1,0:T(8,128)S(1)} %get-tuple-element.345), channel_id=1, replica_groups=mesh['cell'=32,'blk'=16] {'cell'}, use_global_device_ids=true, to_apply=%region_1.0 | all-reduce | flops 1024 | bytes 8192 | tf_op jit(solution)/shard_map/while/body/eval_jaxpr/psum | solution.py:58
  126.9 124.2 %while.38 = (s32[]{:T(128)}, f32[32,32]{1,0:T(8,128)S(1)}, f32[32,32]{0,1:T(8,128)S(1)}, s32[31,32]{1,0:T(8,128)}, s32[]{:T(128)}) while((s32[]{:T(128)}, f32[32,32]{1,0:T(8,128)S(1)}, f32[32,32]{0,1:T(8,128)S(1)}, s32[31,32]{1,0:T(8,128)}, s32[]{:T(128)}) %tuple.77), condition=%wide.region_5.5_spmd.clone.clone, body=%wide.region_2.4_spmd.clone.clone.sunk | while | flops 1202530 | bytes 61137 | solution.py:42
  260.6 125.0 %psum.18 = f32[32,32]{1,0:T(8,128)S(1)} all-reduce(f32[32,32]{1,0:T(8,128)S(1)} %get-tuple-element.345), channel_id=1, replica_groups=mesh['cell'=32,'blk'=16] {'cell'}, use_global_device_ids=true, to_apply=%region_1.0 | all-reduce | flops 1024 | bytes 8192 | tf_op jit(solution)/shard_map/while/body/eval_jaxpr/psum | solution.py:58
  385.6 124.2 %while.38 = (s32[]{:T(128)}, f32[32,32]{1,0:T(8,128)S(1)}, f32[32,32]{0,1:T(8,128)S(1)}, s32[31,32]{1,0:T(8,128)}, s32[]{:T(128)}) while((s32[]{:T(128)}, f32[32,32]{1,0:T(8,128)S(1)}, f32[32,32]{0,1:T(8,128)S(1)}, s32[31,32]{1,0:T(8,128)}, s32[]{:T(128)}) %tuple.77), condition=%wide.region_5.5_spmd.clone.clone, body=%wide.region_2.4_spmd.clone.clone.sunk | while | flops 1202530 | bytes 61137 | solution.py:42
  515.7 5.1 collective-permute-done.1
  521.2 124.9 %psum.18 = f32[32,32]{1,0:T(8,128)S(1)} all-reduce(f32[32,32]{1,0:T(8,128)S(1)} %get-tuple-element.345), channel_id=1, replica_groups=mesh['cell'=32,'blk'=16] {'cell'}, use_global_device_ids=true, to_apply=%region_1.0 | all-reduce | flops 1024 | bytes 8192 | tf_op jit(solution)/shard_map/while/body/eval_jaxpr/psum | solution.py:58
  646.1 124.2 %while.38 = (s32[]{:T(128)}, f32[32,32]{1,0:T(8,128)S(1)}, f32[32,32]{0,1:T(8,128)S(1)}, s32[31,32]{1,0:T(8,128)}, s32[]{:T(128)}) while((s32[]{:T(128)}, f32[32,32]{1,0:T(8,128)S(1)}, f32[32,32]{0,1:T(8,128)S(1)}, s32[31,32]{1,0:T(8,128)}, s32[]{:T(128)}) %tuple.77), condition=%wide.region_5.5_spmd.clone.clone, body=%wide.region_2.4_spmd.clone.clone.sunk | while | flops 1202530 | bytes 61137 | solution.py:42
  770.7 4.9 collective-permute-start
  777.5 4.1 collective-permute-done.1
  782.0 124.9 %psum.18 = f32[32,32]{1,0:T(8,128)S(1)} all-reduce(f32[32,32]{1,0:T(8,128)S(1)} %get-tuple-element.345), channel_id=1, replica_groups=mesh['cell'=32,'blk'=16] {'cell'}, use_global_device_ids=true, to_apply=%region_1.0 | all-reduce | flops 1024 | bytes 8192 | tf_op jit(solution)/shard_map/while/body/eval_jaxpr/psum | solution.py:58
  906.9 124.2 %while.38 = (s32[]{:T(128)}, f32[32,32]{1,0:T(8,128)S(1)}, f32[32,32]{0,1:T(8,128)S(1)}, s32[31,32]{1,0:T(8,128)}, s32[]{:T(128)}) while((s32[]{:T(128)}, f32[32,32]{1,0:T(8,128)S(1)}, f32[32,32]{0,1:T(8,128)S(1)}, s32[31,32]{1,0:T(8,128)}, s32[]{:T(128)}) %tuple.77), condition=%wide.region_5.5_spmd.clone.clone, body=%wide.region_2.4_spmd.clone.clone.sunk | while | flops 1202530 | bytes 61137 | solution.py:42
  1041.4 125.0 %psum.18 = f32[32,32]{1,0:T(8,128)S(1)} all-reduce(f32[32,32]{1,0:T(8,128)S(1)} %get-tuple-element.345), channel_id=1, replica_groups=mesh['cell'=32,'blk'=16] {'cell'}, use_global_device_ids=true, to_apply=%region_1.0 | all-reduce | flops 1024 | bytes 8192 | tf_op jit(solution)/shard_map/while/body/eval_jaxpr/psum | solution.py:58
  1166.4 124.2 %while.38 = (s32[]{:T(128)}, f32[32,32]{1,0:T(8,128)S(1)}, f32[32,32]{0,1:T(8,128)S(1)}, s32[31,32]{1,0:T(8,128)}, s32[]{:T(128)}) while((s32[]{:T(128)}, f32[32,32]{1,0:T(8,128)S(1)}, f32[32,32]{0,1:T(8,128)S(1)}, s32[31,32]{1,0:T(8,128)}, s32[]{:T(128)}) %tuple.77), condition=%wide.region_5.5_spmd.clone.clone, body=%wide.region_2.4_spmd.clone.clone.sunk | while | flops 1202530 | bytes 61137 | solution.py:42
  1291.0 4.5 collective-permute-start
  1297.4 4.1 collective-permute-done.1
  1301.9 124.9 %psum.18 = f32[32,32]{1,0:T(8,128)S(1)} all-reduce(f32[32,32]{1,0:T(8,128)S(1)} %get-tuple-element.345), channel_id=1, replica_groups=mesh['cell'=32,'blk'=16] {'cell'}, use_global_device_ids=true, to_apply=%region_1.0 | all-reduce | flops 1024 | bytes 8192 | tf_op jit(solution)/shard_map/while/body/eval_jaxpr/psum | solution.py:58
  1426.8 124.2 %while.38 = (s32[]{:T(128)}, f32[32,32]{1,0:T(8,128)S(1)}, f32[32,32]{0,1:T(8,128)S(1)}, s32[31,32]{1,0:T(8,128)}, s32[]{:T(128)}) while((s32[]{:T(128)}, f32[32,32]{1,0:T(8,128)S(1)}, f32[32,32]{0,1:T(8,128)S(1)}, s32[31,32]{1,0:T(8,128)}, s32[]{:T(128)}) %tuple.77), condition=%wide.region_5.5_spmd.clone.clone, body=%wide.region_2.4_spmd.clone.clone.sunk | while | flops 1202530 | bytes 61137 | solution.py:42
  1551.4 4.9 collective-permute-start
  1558.2 4.1 collective-permute-done.1
  1562.7 124.9 %psum.18 = f32[32,32]{1,0:T(8,128)S(1)} all-reduce(f32[32,32]{1,0:T(8,128)S(1)} %get-tuple-element.345), channel_id=1, replica_groups=mesh['cell'=32,'blk'=16] {'cell'}, use_global_device_ids=true, to_apply=%region_1.0 | all-reduce | flops 1024 | bytes 8192 | tf_op jit(solution)/shard_map/while/body/eval_jaxpr/psum | solution.py:58
  1687.6 124.2 %while.38 = (s32[]{:T(128)}, f32[32,32]{1,0:T(8,128)S(1)}, f32[32,32]{0,1:T(8,128)S(1)}, s32[31,32]{1,0:T(8,128)}, s32[]{:T(128)}) while((s32[]{:T(128)}, f32[32,32]{1,0:T(8,128)S(1)}, f32[32,32]{0,1:T(8,128)S(1)}, s32[31,32]{1,0:T(8,128)}, s32[]{:T(128)}) %tuple.77), condition=%wide.region_5.5_spmd.clone.clone, body=%wide.region_2.4_spmd.clone.clone.sunk | while | flops 1202530 | bytes 61137 | solution.py:42
  1817.7 4.1 collective-permute-done.1
  1823.1 68.8 %psum.16 = f32[32]{0:T(128)S(1)} all-reduce(f32[32]{0:T(128)S(1)} %get-tuple-element.224), channel_id=1, replica_groups=mesh['cell'=32,'blk'=16] {'cell'}, use_global_device_ids=true, to_apply=%region_8.9 | all-reduce | flops 32 | bytes 256 | tf_op jit(solution)/shard_map/psum | solution.py:77
  (2670 shorter events, 900.3 us)
Async XLA Ops:
  251.5 4.7 collective-permute-start
  254.3 5.9 collective-permute-start.1
  510.2 5.5 collective-permute-start
  513.8 7.0 collective-permute-start.1
  770.7 6.8 collective-permute-start
  775.5 6.0 collective-permute-start.1
  1031.4 5.6 collective-permute-start
  1035.1 5.9 collective-permute-start.1
  1291.0 6.4 collective-permute-start
  1295.5 6.0 collective-permute-start.1
  1551.4 6.8 collective-permute-start
  1556.2 6.0 collective-permute-start.1
  1812.2 5.6 collective-permute-start
  1815.8 6.0 collective-permute-start.1
where the time goes:
time: 1920 us; the launch traced here: 1890 us
  blocking collectives  943 us (49%)
  other arithmetic  370 us (19%)
  local copies, waits for them, and re-layouts  324 us (17%)
  matrix products  171 us (9%)
  starting transfers between devices  36.9 us (2%)
  waiting for transfers between devices  33.7 us (2%)
    psum x7, blocking collectives, round_step(): gram_whole = lax.psum(gram_local, 'cell')  875 us
    cos x217, other arithmetic, one_step(): cosine = jnp.cos(angles)  167 us
    select_n x217, other arithmetic, one_step(): sine_part = jnp.where(is_lower, jnp.sin(angles), -jnp.sin(angles))  159 us
    gather x217, local copies, waits for them, and re-layouts, one_step(): own_diag = jnp.diagonal(symmetric)  156 us
    eq x217, local copies, waits for them, and re-layouts, one_step(): onehot = (partner[:, None] == positions[None, :]).astype(jnp.float32)  151 us
    psum x1, blocking collectives, on_device(): mode_energy = lax.psum(energy_local, 'cell') / total_rows  68.8 us
    dot_general x217, matrix products, one_step(): jnp.dot(accumulated, rotation_step, precision=lax.Precision.HIGHEST)  60.8 us
    dot_general x217, matrix products, one_step(): jnp.dot(rotation_step.T, gram_now, precision=lax.Precision.HIGHEST)  60.1 us
  transfers between devices with their start and end apart: 14, of which 14 were waited for; matrix products, arithmetic and copies ran while one was open for 0% of the time, Pallas kernels for 0%

commit v1 on v0

--- a/solution.py
+++ b/solution.py
@@ -74,7 +74,7 @@
     squared = current * current
     energy_local = jnp.sum(squared, axis=1)
     total_rows = local_rows * lax.axis_size("cell")
-    mode_energy = lax.psum(energy_local, "cell") / total_rows
+    mode_energy = jnp.sum(lax.all_gather(energy_local, "cell"), axis=0) / total_rows
     return (squared, mode_energy)
 
 

time: 1920 us -> 1920 us (level)
    unnamed x0 -> x1, blocking collectives: none -> 68.8 us
    psum x1 -> x0, blocking collectives: 68.8 us -> none  [on_device(): mode_energy = lax.psum(energy_local, 'cell') / total_rows]
where the time goes in v1:
time: 1920 us; the launch traced here: 1890 us
  blocking collectives  944 us (49%)
  other arithmetic  370 us (19%)
  local copies, waits for them, and re-layouts  325 us (17%)
  matrix products  170 us (9%)
  starting transfers between devices  36.9 us (2%)
  waiting for transfers between devices  33.7 us (2%)
    psum x7, blocking collectives, round_step(): gram_whole = lax.psum(gram_local, 'cell')  875 us
    cos x217, other arithmetic, one_step(): cosine = jnp.cos(angles)  167 us
    select_n x217, other arithmetic, one_step(): sine_part = jnp.where(is_lower, jnp.sin(angles), -jnp.sin(angles))  159 us
    gather x217, local copies, waits for them, and re-layouts, one_step(): own_diag = jnp.diagonal(symmetric)  155 us
    eq x217, local copies, waits for them, and re-layouts, one_step(): onehot = (partner[:, None] == positions[None, :]).astype(jnp.float32)  151 us
    unnamed x1, blocking collectives  68.8 us
    dot_general x217, matrix products, one_step(): jnp.dot(accumulated, rotation_step, precision=lax.Precision.HIGHEST)  60.1 us
    dot_general x217, matrix products, one_step(): jnp.dot(rotation_step.T, gram_now, precision=lax.Precision.HIGHEST)  60.1 us
  transfers between devices with their start and end apart: 14, of which 14 were waited for; matrix products, arithmetic and copies ran while one was open for 0% of the time, Pallas kernels for 0%

profile of v1, /device:TPU:1, one launch (start us, length us, event | category | flops | bytes accessed | tf_op | source)
XLA Modules:
  0.0 1893.9 jit_solution(2610574861932456558)
XLA Ops:
  1.9 1819.4 %while.37 = (s32[]{:T(128)}, f32[32,2048]{1,0:T(8,128)S(1)}, f32[32,32]{1,0:T(8,128)S(1)}, pred[]{:T(512)}, s32[31,32]{1,0:T(8,128)}, /*index=5*/pred[]{:T(512)}, s32[]{:T(128)}, s32[]{:T(128)}, s32[]{:T(128)}) while((s32[]{:T(128)}, f32[32,2048]{1,0:T(8,128)S(1)}, f32[32,32]{1,0:T(8,128)S(1)}, pred[]{:T(512)}, s32[31,32]{1,0:T(8,128)}, ...), condition=%wide.region_6.7_spmd, body=%wide.region_0.6_spmd.sunk | while | flops 51701092 | bytes 3620777 | solution.py:73
  2.0 125.0 %psum.10 = f32[32,32]{1,0:T(8,128)S(1)} all-reduce(f32[32,32]{1,0:T(8,128)S(1)} %get-tuple-element.345), channel_id=1, replica_groups=mesh['cell'=32,'blk'=16] {'cell'}, use_global_device_ids=true, to_apply=%region_1.0 | all-reduce | flops 1024 | bytes 8192 | tf_op jit(solution)/shard_map/while/body/eval_jaxpr/psum | solution.py:58
  126.9 124.0 %while.38 = (s32[]{:T(128)}, f32[32,32]{1,0:T(8,128)S(1)}, f32[32,32]{0,1:T(8,128)S(1)}, s32[31,32]{1,0:T(8,128)}, s32[]{:T(128)}) while((s32[]{:T(128)}, f32[32,32]{1,0:T(8,128)S(1)}, f32[32,32]{0,1:T(8,128)S(1)}, s32[31,32]{1,0:T(8,128)}, s32[]{:T(128)}) %tuple.77), condition=%wide.region_5.5_spmd.clone.clone, body=%wide.region_2.4_spmd.clone.clone.sunk | while | flops 1202530 | bytes 61129 | solution.py:42
  260.5 125.0 %psum.10 = f32[32,32]{1,0:T(8,128)S(1)} all-reduce(f32[32,32]{1,0:T(8,128)S(1)} %get-tuple-element.345), channel_id=1, replica_groups=mesh['cell'=32,'blk'=16] {'cell'}, use_global_device_ids=true, to_apply=%region_1.0 | all-reduce | flops 1024 | bytes 8192 | tf_op jit(solution)/shard_map/while/body/eval_jaxpr/psum | solution.py:58
  385.5 124.0 %while.38 = (s32[]{:T(128)}, f32[32,32]{1,0:T(8,128)S(1)}, f32[32,32]{0,1:T(8,128)S(1)}, s32[31,32]{1,0:T(8,128)}, s32[]{:T(128)}) while((s32[]{:T(128)}, f32[32,32]{1,0:T(8,128)S(1)}, f32[32,32]{0,1:T(8,128)S(1)}, s32[31,32]{1,0:T(8,128)}, s32[]{:T(128)}) %tuple.77), condition=%wide.region_5.5_spmd.clone.clone, body=%wide.region_2.4_spmd.clone.clone.sunk | while | flops 1202530 | bytes 61129 | solution.py:42
  515.4 5.1 collective-permute-done.1
  521.0 124.9 %psum.10 = f32[32,32]{1,0:T(8,128)S(1)} all-reduce(f32[32,32]{1,0:T(8,128)S(1)} %get-tuple-element.345), channel_id=1, replica_groups=mesh['cell'=32,'blk'=16] {'cell'}, use_global_device_ids=true, to_apply=%region_1.0 | all-reduce | flops 1024 | bytes 8192 | tf_op jit(solution)/shard_map/while/body/eval_jaxpr/psum | solution.py:58
  645.9 124.0 %while.38 = (s32[]{:T(128)}, f32[32,32]{1,0:T(8,128)S(1)}, f32[32,32]{0,1:T(8,128)S(1)}, s32[31,32]{1,0:T(8,128)}, s32[]{:T(128)}) while((s32[]{:T(128)}, f32[32,32]{1,0:T(8,128)S(1)}, f32[32,32]{0,1:T(8,128)S(1)}, s32[31,32]{1,0:T(8,128)}, s32[]{:T(128)}) %tuple.77), condition=%wide.region_5.5_spmd.clone.clone, body=%wide.region_2.4_spmd.clone.clone.sunk | while | flops 1202530 | bytes 61129 | solution.py:42
  770.3 4.9 collective-permute-start
  777.1 4.1 collective-permute-done.1
  781.6 124.9 %psum.10 = f32[32,32]{1,0:T(8,128)S(1)} all-reduce(f32[32,32]{1,0:T(8,128)S(1)} %get-tuple-element.345), channel_id=1, replica_groups=mesh['cell'=32,'blk'=16] {'cell'}, use_global_device_ids=true, to_apply=%region_1.0 | all-reduce | flops 1024 | bytes 8192 | tf_op jit(solution)/shard_map/while/body/eval_jaxpr/psum | solution.py:58
  906.5 124.0 %while.38 = (s32[]{:T(128)}, f32[32,32]{1,0:T(8,128)S(1)}, f32[32,32]{0,1:T(8,128)S(1)}, s32[31,32]{1,0:T(8,128)}, s32[]{:T(128)}) while((s32[]{:T(128)}, f32[32,32]{1,0:T(8,128)S(1)}, f32[32,32]{0,1:T(8,128)S(1)}, s32[31,32]{1,0:T(8,128)}, s32[]{:T(128)}) %tuple.77), condition=%wide.region_5.5_spmd.clone.clone, body=%wide.region_2.4_spmd.clone.clone.sunk | while | flops 1202530 | bytes 61129 | solution.py:42
  1041.0 125.0 %psum.10 = f32[32,32]{1,0:T(8,128)S(1)} all-reduce(f32[32,32]{1,0:T(8,128)S(1)} %get-tuple-element.345), channel_id=1, replica_groups=mesh['cell'=32,'blk'=16] {'cell'}, use_global_device_ids=true, to_apply=%region_1.0 | all-reduce | flops 1024 | bytes 8192 | tf_op jit(solution)/shard_map/while/body/eval_jaxpr/psum | solution.py:58
  1166.0 124.0 %while.38 = (s32[]{:T(128)}, f32[32,32]{1,0:T(8,128)S(1)}, f32[32,32]{0,1:T(8,128)S(1)}, s32[31,32]{1,0:T(8,128)}, s32[]{:T(128)}) while((s32[]{:T(128)}, f32[32,32]{1,0:T(8,128)S(1)}, f32[32,32]{0,1:T(8,128)S(1)}, s32[31,32]{1,0:T(8,128)}, s32[]{:T(128)}) %tuple.77), condition=%wide.region_5.5_spmd.clone.clone, body=%wide.region_2.4_spmd.clone.clone.sunk | while | flops 1202530 | bytes 61129 | solution.py:42
  1290.4 4.5 collective-permute-start
  1296.8 4.1 collective-permute-done.1
  1301.3 124.9 %psum.10 = f32[32,32]{1,0:T(8,128)S(1)} all-reduce(f32[32,32]{1,0:T(8,128)S(1)} %get-tuple-element.345), channel_id=1, replica_groups=mesh['cell'=32,'blk'=16] {'cell'}, use_global_device_ids=true, to_apply=%region_1.0 | all-reduce | flops 1024 | bytes 8192 | tf_op jit(solution)/shard_map/while/body/eval_jaxpr/psum | solution.py:58
  1426.3 124.0 %while.38 = (s32[]{:T(128)}, f32[32,32]{1,0:T(8,128)S(1)}, f32[32,32]{0,1:T(8,128)S(1)}, s32[31,32]{1,0:T(8,128)}, s32[]{:T(128)}) while((s32[]{:T(128)}, f32[32,32]{1,0:T(8,128)S(1)}, f32[32,32]{0,1:T(8,128)S(1)}, s32[31,32]{1,0:T(8,128)}, s32[]{:T(128)}) %tuple.77), condition=%wide.region_5.5_spmd.clone.clone, body=%wide.region_2.4_spmd.clone.clone.sunk | while | flops 1202530 | bytes 61129 | solution.py:42
  1550.7 4.9 collective-permute-start
  1557.5 4.1 collective-permute-done.1
  1562.0 124.9 %psum.10 = f32[32,32]{1,0:T(8,128)S(1)} all-reduce(f32[32,32]{1,0:T(8,128)S(1)} %get-tuple-element.345), channel_id=1, replica_groups=mesh['cell'=32,'blk'=16] {'cell'}, use_global_device_ids=true, to_apply=%region_1.0 | all-reduce | flops 1024 | bytes 8192 | tf_op jit(solution)/shard_map/while/body/eval_jaxpr/psum | solution.py:58
  1686.9 124.0 %while.38 = (s32[]{:T(128)}, f32[32,32]{1,0:T(8,128)S(1)}, f32[32,32]{0,1:T(8,128)S(1)}, s32[31,32]{1,0:T(8,128)}, s32[]{:T(128)}) while((s32[]{:T(128)}, f32[32,32]{1,0:T(8,128)S(1)}, f32[32,32]{0,1:T(8,128)S(1)}, s32[31,32]{1,0:T(8,128)}, s32[]{:T(128)}) %tuple.77), condition=%wide.region_5.5_spmd.clone.clone, body=%wide.region_2.4_spmd.clone.clone.sunk | while | flops 1202530 | bytes 61129 | solution.py:42
  1816.9 4.1 collective-permute-done.1
  1824.4 68.8 %all-reduce = f32[1024]{0:T(1024)S(1)} all-reduce(f32[1024]{0:T(1024)S(1)} %dynamic-update-slice), channel_id=2, replica_groups=mesh['cell'=32,'blk'=16] {'cell'}, use_global_device_ids=true, to_apply=%add | all-reduce | flops 1024 | bytes 8192
  (2675 shorter events, 900.2 us)
Async XLA Ops:
  251.3 4.7 collective-permute-start
  254.2 5.9 collective-permute-start.1
  510.0 5.5 collective-permute-start
  513.5 7.0 collective-permute-start.1
  770.3 6.8 collective-permute-start
  775.2 6.0 collective-permute-start.1
  1031.0 5.6 collective-permute-start
  1034.6 5.9 collective-permute-start.1
  1290.4 6.4 collective-permute-start
  1294.9 6.0 collective-permute-start.1
  1550.7 6.8 collective-permute-start
  1555.5 6.0 collective-permute-start.1
  1811.3 5.6 collective-permute-start
  1815.0 6.0 collective-permute-start.1
